TPU v7x, 32 devices: a whole 2x2x4 slice. The times are simulated.
32 devices in a mesh: ia: 2 (over x), ja: 4 (over z), ka: 4 (over y, core).
Axes of the slice: x: 2, y: 2, z: 4, core: 2. Of those that a mesh axis runs over, the one named last changes fastest.
Arguments:
- flow_state: float32 [5, 4, 64, 64, 128], P(None, 'ka', 'ia', 'ja'), may hold values from -6 to 6
- spectral: float32 [3, 4, 64, 64, 128], P(None, 'ka', 'ia', 'ja'), may hold values from 0.5 to 50
- wave_speed: float32 [3, 4, 5], P(None, 'ka'), may hold values from 0.05 to 2
- left_map: float32 [4, 5, 5], P('ka')
- right_map: float32 [4, 5, 5], P('ka')
- donor_block: int32 [32, 32, 1], P(('ia', 'ja', 'ka')), may hold values from 0 to 127
- receiver_block: int32 [32, 32, 1], P(('ia', 'ja', 'ka')), may hold values from 0 to 127, as said below
- fringe_count: int32 [32, 32], P(('ia', 'ja', 'ka')), may hold values from 0 to 1, as said below
- fringe_weight: float32 [3, 32, 32, 1], P(None, ('ia', 'ja', 'ka')), may hold values from 0 to 1
Outputs:
- advanced: float32 [5, 4, 64, 64, 128], P(None, 'ka', 'ia', 'ja')
- increment: float32 [5, 4, 64, 64, 128], P(None, 'ka', 'ia', 'ja')
Inputs may be any that keep to these rules, and one draw needn't show every extreme that they name: `receiver_block`: on each receiving device the cube numbers over all sources and slots are distinct. `fringe_count`: in every draw some receiving device has 1 live slots from every source.
All inputs are finite; a program needn't handle non-finite values.
Results may differ from a plain program's by a relative error of at most 0.0003.
Values sent between devices are 32-bit elements; how exact they have to be, the bound alone decides.
A program may use at most 128 MiB of HBM per device.

v0:
```python
import functools
import math

import jax
import jax.numpy as jnp
from jax import lax
from jax.experimental import pallas as pl
from jax.experimental.pallas import tpu as pltpu
from jax.sharding import PartitionSpec as P

BS = 8
LANES = 128
GROUPS = LANES // BS
QUARTER = 0.25
VMEM = pl.BlockSpec(memory_space=pltpu.VMEM)
SMEM = pl.BlockSpec(memory_space=pltpu.SMEM)
F32 = jnp.float32


def call(body, outs, ins, args, scratch=(), flops=4_000_000, collective_id=None):
    moved = sum(a.size * 4 for a in args) + sum(o.size * 4 for o in outs)
    held = sum(math.prod(r.shape) * 4 for r in scratch if math.prod(r.shape) > 1024)
    options = {} if collective_id is None else {"collective_id": collective_id, "has_side_effects": True}
    return pl.pallas_call(
        body,
        out_shape=outs,
        in_specs=ins,
        out_specs=[VMEM] * len(outs),
        scratch_shapes=list(scratch),
        compiler_params=pltpu.CompilerParams(vmem_limit_bytes=moved + held + (3 << 20), **options),
        cost_estimate=pl.CostEstimate(flops=flops, bytes_accessed=moved, transcendentals=0),
    )(*args)


def shape(*dims):
    return jax.ShapeDtypeStruct(dims, F32)


def lane_iota():
    return lax.broadcasted_iota(jnp.int32, (BS, LANES), 1)


def groups_turned(tiles):
    group = lane_iota() // BS
    tiles = list(tiles)
    distance = 1
    while distance < GROUPS:
        upper = (group // distance) % 2 == 1
        shift = distance * BS
        for a in range(GROUPS):
            if a & distance == 0:
                x, y = tiles[a], tiles[a + distance]
                tiles[a] = jnp.where(upper, pltpu.roll(y, shift, 1), x)
                tiles[a + distance] = jnp.where(upper, y, pltpu.roll(x, LANES - shift, 1))
        distance *= 2
    return tiles


def tile_at(block, rows_j, g):
    blocks_j = rows_j // BS
    row = (block // blocks_j) * (BS * rows_j) + (block % blocks_j) * BS + (g % BS) * rows_j
    return pl.ds(pl.multiple_of(row, BS), BS)


def pack_all(rows_j, flow, packed):
    groups = flow.shape[0] * BS

    def one(block, carry):
        for first in range(0, groups, GROUPS):
            count = min(GROUPS, groups - first)
            tiles = [flow[g // BS, tile_at(block, rows_j, g), :] for g in range(first, first + count)]
            tiles = groups_turned(tiles + tiles[:1] * (GROUPS - count))
            q = first // GROUPS
            for k in range(GROUPS):
                packed[block * GROUPS + k, q * BS : (q + 1) * BS, :] = tiles[k]
        return carry

    lax.fori_loop(0, packed.shape[0] // GROUPS, one, 0)


def unpack_all(rows_j, source, packed, arrived, filled):
    groups = filled.shape[0] * BS

    def one(block, carry):
        for first in range(0, groups, GROUPS):
            q = first // GROUPS
            tiles = []
            for k in range(GROUPS):
                slot = source[block * GROUPS + k]
                live = jnp.full((BS, LANES), slot, jnp.int32) >= 0
                fresh = arrived[jnp.maximum(slot, 0), q * BS : (q + 1) * BS, :]
                kept = packed[block * GROUPS + k, q * BS : (q + 1) * BS, :]
                tiles.append(jnp.where(live, fresh, kept))
            tiles = groups_turned(tiles)
            for g in range(first, min(first + GROUPS, groups)):
                filled[g // BS, tile_at(block, rows_j, g), :] = tiles[g - first]
        return carry

    lax.fori_loop(0, packed.shape[0] // GROUPS, one, 0)


def blend(cubes, shifted, weight):
    return (1.0 - weight) * cubes + weight * shifted


def interpolate_all(weights, arrived):
    slots, packed_rows, lanes = arrived.shape
    lane = lax.broadcasted_iota(jnp.int32, (packed_rows, LANES), 1)
    row = lax.broadcasted_iota(jnp.int32, (packed_rows, LANES), 0)

    def one(slot, carry):
        cubes = arrived[slot]
        after = jnp.where(lane % (BS * BS) >= BS * (BS - 1), cubes, pltpu.roll(cubes, LANES - BS, 1))
        cubes = blend(cubes, after, weights[slot])
        after = jnp.where(row % BS == BS - 1, cubes, pltpu.roll(cubes, packed_rows - 1, 0))
        cubes = blend(cubes, after, weights[slots + slot])
        after = jnp.where(lane % BS == BS - 1, cubes, pltpu.roll(cubes, LANES - 1, 1))
        arrived[slot] = blend(cubes, after, weights[2 * slots + slot])
        return carry

    lax.fori_loop(0, slots, one, 0, unroll=4)


def eliminate(coupling, older_first, older_second, last_first, last_second):
    fourth = QUARTER * coupling
    coupled = -coupling + fourth * older_first
    pivots = 1.0 + 2.5 * coupling + fourth * older_second - last_first * coupled
    inverse = 1.0 / pivots
    first = (-coupling - last_second * coupled) * inverse
    second = -fourth * inverse
    return inverse, coupled * inverse, first, second


def meet(gains, values, far_gains, far_values):
    f0, s0, f1, s1 = gains
    g0, t0, g1, t1 = far_gains
    r0, r1 = values
    q0, q1 = far_values
    cross = g1 - t1 * f0
    a11 = 1.0 - t1 * s0 - cross * f1
    a12 = -cross * s1
    b1 = q1 - t1 * r0 - cross * r1
    a21 = g0 - t0 * f1
    a22 = 1.0 - t0 * s1
    b2 = q0 - t0 * r1
    scale = 1.0 / (a11 * a22 - a12 * a21)
    return (b1 * a22 - a12 * b2) * scale, (a11 * b2 - a21 * b1) * scale


def row_of(n, count, lower):
    return jnp.where(lower, n, count - 1 - n)


def factor_pass(direction, rows, stride, is_lower, speeds, spectral, start, outs, last):
    inverse, coupled, first, second = outs
    variables, total, lanes = inverse.shape
    plane = total // rows

    def one(n, carry):
        row = row_of(n, rows, is_lower)
        at = pl.ds(pl.multiple_of(row * plane, BS), plane)
        if stride is None:
            rho = spectral[direction, at, :]
        else:
            rho = spectral[direction, pl.ds(row, plane, stride=stride), :]
        fresh = []
        for v in range(variables):
            older_first, older_second, last_first, last_second = carry[v]
            a, b, c, d = eliminate(
                speeds[direction * variables + v] * rho, older_first, older_second, last_first, last_second
            )
            inverse[v, at, :] = a
            coupled[v, at, :] = b
            first[v, at, :] = c
            second[v, at, :] = d
            fresh.append((last_first, last_second, c, d))
        return tuple(fresh)

    begin = tuple(tuple(start[m, v] for m in range(4)) for v in range(variables))
    ends = lax.fori_loop(0, rows, one, begin)
    for v in range(variables):
        for m in range(4):
            last[m, v] = ends[v][m]


class Line:
    def __init__(self, axis):
        self.axis = axis
        self.members = lax.axis_size(axis)
        self.half = self.members // 2
        self.place = lax.axis_index(axis)
        self.lower = self.place < self.half
        self.depth = jnp.where(self.lower, self.place, self.members - 1 - self.place)
        self.inner = jnp.where(self.lower, self.place + 1, self.place - 1)
        self.outer = jnp.where(self.lower, self.place - 1, self.place + 1)
        self.middle = self.depth == self.half - 1
        self.end = self.depth == 0

    def send(self, source, target, sems, device):
        return pltpu.make_async_remote_copy(
            src_ref=source,
            dst_ref=target,
            send_sem=sems.at[0],
            recv_sem=sems.at[1],
            device_id={self.axis: device},
            device_id_type=pl.DeviceIdType.MESH,
        )


def take_start(line, source, start, sems):
    @pl.when(line.end)
    def _():
        start[...] = jnp.zeros(start.shape, F32)

    if line.half > 1:

        @pl.when(jnp.logical_not(line.end))
        def _():
            line.send(source, start, sems, line.inner).wait_recv()


def send_inward(line, source, start, start_sems, far, far_sems):
    if line.half > 1:

        @pl.when(jnp.logical_not(line.middle))
        def _():
            line.send(source, start, start_sems, line.inner).start()

    @pl.when(line.middle)
    def _():
        line.send(source, far, far_sems, line.inner).start()


def end_inward(line, source, start, start_sems, far, far_sems):
    if line.half > 1:

        @pl.when(jnp.logical_not(line.middle))
        def _():
            line.send(source, start, start_sems, line.inner).wait_send()

    @pl.when(line.middle)
    def _():
        line.send(source, far, far_sems, line.inner).wait_send()


def peer_of(number, axes):
    rest, place = number, {}
    for axis in reversed(axes):
        place[axis] = rest % lax.axis_size(axis)
        rest = rest // lax.axis_size(axis)
    return place


def residual_pass(
    rows_i, is_lower, left, padded, spectral, j_before, j_after, inverse, coupled, second, start, reduced, last
):
    variables, total, lanes = inverse.shape
    rows_j = total // rows_i
    lane = lax.broadcasted_iota(jnp.int32, (rows_j, lanes), 1)
    row_id = lax.broadcasted_iota(jnp.int32, (rows_j, lanes), 0)

    def one(n, carry):
        row = row_of(n, rows_i, is_lower)
        base = pl.multiple_of(row * rows_j, BS)
        at = pl.ds(base, rows_j)
        rho = [spectral[e, at, :] for e in range(3)]
        residual = []
        for v in range(variables):
            center = padded[v, pl.ds(base + rows_j, rows_j), :]
            twice = 2.0 * center
            along_i = padded[v, pl.ds(base + 2 * rows_j, rows_j), :] + padded[v, at, :] - twice
            after = jnp.where(
                row_id == rows_j - 1, j_after[v, pl.ds(row, 1), :], pltpu.roll(center, rows_j - 1, 0)
            )
            before = jnp.where(row_id == 0, j_before[v, pl.ds(row, 1), :], pltpu.roll(center, 1, 0))
            along_j = after + before - twice
            after = jnp.where(lane == lanes - 1, 0.0, pltpu.roll(center, lanes - 1, 1))
            before = jnp.where(lane == 0, 0.0, pltpu.roll(center, 1, 1))
            along_k = after + before - twice
            residual.append(rho[0] * along_i + rho[1] * along_j + rho[2] * along_k)
        fresh = []
        for v in range(variables):
            source = left[v * variables] * residual[0]
            for u in range(1, variables):
                source = source + left[v * variables + u] * residual[u]
            older, newer = carry[v]
            value = source * inverse[v, at, :] - second[v, at, :] * older - coupled[v, at, :] * newer
            reduced[v, at, :] = value
            fresh.append((newer, value))
        return tuple(fresh)

    ends = lax.fori_loop(0, rows_i, one, begin_of(start, variables))
    for v in range(variables):
        last[0, v] = ends[v][0]
        last[1, v] = ends[v][1]


def forward_pass(rows, is_lower, source, inverse, coupled, second, start, reduced, last):
    variables, total, lanes = source.shape
    plane = total // rows

    def one(n, carry):
        at = pl.ds(pl.multiple_of(row_of(n, rows, is_lower) * plane, BS), plane)
        fresh = []
        for v in range(variables):
            older, newer = carry[v]
            value = (
                source[v, at, :] * inverse[v, at, :]
                - second[v, at, :] * older
                - coupled[v, at, :] * newer
            )
            reduced[v, at, :] = value
            fresh.append((newer, value))
        return tuple(fresh)

    begin = tuple((start[0, v], start[1, v]) for v in range(variables))
    ends = lax.fori_loop(0, rows, one, begin)
    for v in range(variables):
        last[0, v] = ends[v][0]
        last[1, v] = ends[v][1]


def backward_pass(rows, is_lower, reduced, first, second, begin, store):
    variables, total, lanes = reduced.shape
    plane = total // rows

    def one(step, carry):
        row = row_of(rows - 1 - step, rows, is_lower)
        at = pl.ds(pl.multiple_of(row * plane, BS), plane)
        fresh = []
        for v in range(variables):
            nearer, farther = carry[v]
            value = reduced[v, at, :] - first[v, at, :] * nearer - second[v, at, :] * farther
            store(v, row, value)
            fresh.append((value, nearer))
        return tuple(fresh)

    return lax.fori_loop(0, rows, one, begin)


def start_values(variables, gains, values, far_gains, far_values):
    return tuple(
        meet(
            [gains[m, v] for m in range(4)],
            [values[m, v] for m in range(2)],
            [far_gains[m, v] for m in range(4)],
            [far_values[m, v] for m in range(2)],
        )
        for v in range(variables)
    )


def begin_of(next_values, variables):
    return tuple((next_values[0, v], next_values[1, v]) for v in range(variables))


def solve_back(line, rows, reduced, gains, last_gains, far_gains, last, far, far_sems, nexts, next_sems, solved, store):
    variables = reduced.shape[0]

    @pl.when(line.middle)
    def _():
        line.send(last, far, far_sems, line.inner).wait_recv()
        for v, pair in enumerate(start_values(variables, last_gains, last, far_gains, far)):
            nexts[0, v] = pair[0]
            nexts[1, v] = pair[1]

    if line.half > 1:

        @pl.when(jnp.logical_not(line.middle))
        def _():
            line.send(solved, nexts, next_sems, line.outer).wait_recv()

    ends = backward_pass(
        rows, line.lower, reduced, gains[2], gains[3], begin_of(nexts, variables), store
    )
    if line.half > 1:
        for v in range(variables):
            solved[0, v] = ends[v][0]
            solved[1, v] = ends[v][1]

        @pl.when(jnp.logical_not(line.end))
        def _():
            line.send(solved, nexts, next_sems, line.outer).start()


def step_body(
    axes, capacity, rows_i, rows_j, speeds, left, right, donor, source, weights, flow, spectral,
    advanced, increment, *refs,
):
    packed, outbound, arrived, filled = refs[:4]
    gains_i, (last_gains_i, far_gains_i, start_gains_i) = refs[4:8], refs[8:11]
    gains_j, (last_gains_j, far_gains_j, start_gains_j) = refs[11:15], refs[15:18]
    sent, got, gain_sems_i, gain_sems_j = refs[18:22]
    (padded, reduced, turned, i_halo, j_edge, j_halo, halo_sems) = refs[22:29]
    ends_i, start_i, far_i, nexts_i, solved_i, sems_i = refs[29:35]
    ends_j, start_j, far_j, nexts_j, solved_j, sems_j = refs[35:41]
    lines, thirds = refs[41], refs[42:]
    variables, total, lanes = flow.shape
    line_i, line_j = Line("ia"), Line("ja")
    devices = 1
    me = 0
    for axis in axes:
        devices = devices * lax.axis_size(axis)
        me = me * lax.axis_size(axis) + lax.axis_index(axis)
    barrier = pltpu.get_barrier_semaphore()

    def greet(step, carry):
        peer = peer_of((me + step) % devices, axes)
        pl.semaphore_signal(barrier, inc=1, device_id=peer, device_id_type=pl.DeviceIdType.MESH)
        return carry

    lax.fori_loop(1, devices, greet, 0)
    pack_all(rows_j, flow, packed)

    def gather(slot, carry):
        outbound[slot] = packed[donor[slot]]
        return carry

    lax.fori_loop(0, devices * capacity, gather, 0, unroll=4)
    pl.semaphore_wait(barrier, devices - 1)

    def slots(device):
        return pl.ds(device * capacity, capacity)

    def cubes(step, to, of):
        return pltpu.make_async_remote_copy(
            src_ref=outbound.at[slots(to)],
            dst_ref=arrived.at[slots(of)],
            send_sem=sent.at[step],
            recv_sem=got.at[step],
            device_id=peer_of(to, axes),
            device_id_type=pl.DeviceIdType.MESH,
        )

    def begin(step, carry):
        cubes(step, (me + step) % devices, me).start()
        return carry

    lax.fori_loop(1, devices, begin, 0)
    arrived[slots(me)] = outbound[slots(me)]

    for direction, line, rows, stride, gains, last, far, start, sems in (
        (1, line_j, rows_j, rows_j, gains_j, last_gains_j, far_gains_j, start_gains_j, gain_sems_j),
        (0, line_i, rows_i, None, gains_i, last_gains_i, far_gains_i, start_gains_i, gain_sems_i),
    ):
        take_start(line, last, start, sems.at[0])
        factor_pass(direction, rows, stride, line.lower, speeds, spectral, start, gains, last)
        send_inward(line, last, start, sems.at[0], far, sems.at[1])

    def end(step, carry):
        cubes(step, (me + step) % devices, (me + devices - step) % devices).wait_recv()
        return carry

    lax.fori_loop(1, devices, end, 0)
    interpolate_all(weights, arrived)
    unpack_all(rows_j, source, packed, arrived, filled)

    def sides(line):
        return (line.place > 0, line.place - 1), (line.place < line.members - 1, line.place + 1)

    for v in range(variables):
        j_edge[0, v] = filled[v, pl.ds(0, rows_i, stride=rows_j), :]
        j_edge[1, v] = filled[v, pl.ds(rows_j - 1, rows_i, stride=rows_j), :]
    def edges(axis_number, side):
        if axis_number == 1:
            return j_edge.at[side], j_halo.at[1 - side]
        first = 0 if side == 0 else total - rows_j
        return filled.at[:, pl.ds(first, rows_j), :], i_halo.at[1 - side]

    def halo(line, axis_number, side, device):
        source, target = edges(axis_number, side)
        number = axis_number * 2 + side
        return pltpu.make_async_remote_copy(
            src_ref=source,
            dst_ref=target,
            send_sem=halo_sems.at[0, number],
            recv_sem=halo_sems.at[1, number],
            device_id={line.axis: device},
            device_id_type=pl.DeviceIdType.MESH,
        )

    for axis_number, line in ((1, line_j), (0, line_i)):
        for side, (there, device) in enumerate(sides(line)):

            @pl.when(there)
            def _():
                halo(line, axis_number, side, device).start()

    padded[:, rows_j : rows_j + total, :] = filled[...]
    for axis_number, line in ((0, line_i), (1, line_j)):
        for side, (there, device) in enumerate(sides(line)):
            target = (i_halo, j_halo)[axis_number]

            @pl.when(there)
            def _():
                halo(line, axis_number, 1 - side, device).wait_recv()

            @pl.when(jnp.logical_not(there))
            def _():
                target[side] = jnp.zeros(target.shape[1:], F32)

    padded[:, :rows_j, :] = i_halo[0]
    padded[:, rows_j + total :, :] = i_halo[1]

    take_start(line_i, ends_i, start_i, sems_i.at[0])
    residual_pass(
        rows_i, line_i.lower, left, padded, spectral, j_halo.at[0], j_halo.at[1],
        gains_i[0], gains_i[1], gains_i[3], start_i, reduced, ends_i,
    )
    send_inward(line_i, ends_i, start_i, sems_i.at[0], far_i, sems_i.at[1])

    def store_turned(v, row, value):
        turned[v, pl.ds(row, rows_j, stride=rows_i), :] = value

    @pl.when(line_i.middle)
    def _():
        line_i.send(last_gains_i, far_gains_i, gain_sems_i.at[1], line_i.inner).wait_recv()

    solve_back(
        line_i, rows_i, reduced, gains_i, last_gains_i, far_gains_i, ends_i, far_i, sems_i.at[1],
        nexts_i, sems_i.at[2], solved_i, store_turned,
    )

    take_start(line_j, ends_j, start_j, sems_j.at[0])
    forward_pass(
        rows_j, line_j.lower, turned, gains_j[0], gains_j[1], gains_j[3], start_j, reduced, ends_j
    )
    send_inward(line_j, ends_j, start_j, sems_j.at[0], far_j, sems_j.at[1])

    def store_lines(v, row, value):
        lines[v, pl.ds(pl.multiple_of(row * rows_i, BS), rows_i), :] = value

    @pl.when(line_j.middle)
    def _():
        line_j.send(last_gains_j, far_gains_j, gain_sems_j.at[1], line_j.inner).wait_recv()

    solve_back(
        line_j, rows_j, reduced, gains_j, last_gains_j, far_gains_j, ends_j, far_j, sems_j.at[1],
        nexts_j, sems_j.at[2], solved_j, store_lines,
    )

    for axis_number, line in ((0, line_i), (1, line_j)):
        for side, (there, device) in enumerate(sides(line)):

            @pl.when(there)
            def _():
                halo(line, axis_number, side, device).wait_send()

    def close(step, carry):
        cubes(step, (me + step) % devices, me).wait_send()
        return carry

    lax.fori_loop(1, devices, close, 0)
    end_inward(line_i, last_gains_i, start_gains_i, gain_sems_i.at[0], far_gains_i, gain_sems_i.at[1])
    end_inward(line_j, last_gains_j, start_gains_j, gain_sems_j.at[0], far_gains_j, gain_sems_j.at[1])
    for line, ends, start, far, nexts, solved, sems in (
        (line_i, ends_i, start_i, far_i, nexts_i, solved_i, sems_i),
        (line_j, ends_j, start_j, far_j, nexts_j, solved_j, sems_j),
    ):
        end_inward(line, ends, start, sems.at[0], far, sems.at[1])
        if line.half > 1:

            @pl.when(jnp.logical_not(line.end))
            def _():
                line.send(solved, nexts, sems.at[2], line.outer).wait_send()

    finish(rows_j, speeds, right, lines, spectral, filled, advanced, increment, *thirds)


def finish(
    rows_j, speeds, right, lines, spectral, filled,
    advanced, increment, values, coupling, gain_1, gain_2,
):
    variables, total, lanes = lines.shape
    rows_i = total // rows_j
    quarters = total // LANES
    per_quarter = LANES // rows_i
    depth = values.shape[0] // lanes

    for q in range(quarters):
        rho = jnp.concatenate(
            [
                spectral[2, pl.ds(q * per_quarter + j, rows_i, stride=rows_j), :]
                for j in range(per_quarter)
            ],
            axis=0,
        ).T
        for v in range(variables):
            at = pl.ds(v * quarters + q, lanes, stride=depth)
            coupling[at, :] = speeds[2 * variables + v] * rho
            values[at, :] = lines[v, q * LANES : (q + 1) * LANES, :].T
    for spare in range(variables * quarters, depth):
        at = pl.ds(spare, lanes, stride=depth)
        coupling[at, :] = jnp.zeros((lanes, lanes), F32)
        values[at, :] = jnp.zeros((lanes, lanes), F32)

    half = lanes // 2
    gain_1[:depth, :] = jnp.zeros((depth, lanes), F32)
    zero = gain_1[:depth, :]

    def ahead(n, carry):
        fresh = []
        for side in range(2):
            older_first, older_second, older, last_first, last_second, newer = carry[side]
            k = n if side == 0 else lanes - 1 - n
            at = pl.ds(pl.multiple_of(k * depth, BS), depth)
            inverse, coupled, one, two = eliminate(
                coupling[at, :], older_first, older_second, last_first, last_second
            )
            value = values[at, :] * inverse - two * older - coupled * newer
            gain_1[at, :] = one
            gain_2[at, :] = two
            values[at, :] = value
            fresh.append((last_first, last_second, newer, one, two, value))
        return tuple(fresh)

    low, high = lax.fori_loop(0, half, ahead, ((zero,) * 6,) * 2)

    def ends(side):
        return [side[0], side[1], side[3], side[4]], [side[2], side[5]]

    low_next = meet(*ends(low), *ends(high))
    high_next = meet(*ends(high), *ends(low))

    def back(step, carry):
        fresh = []
        for side in range(2):
            nearer, farther = carry[side]
            n = half - 1 - step
            k = n if side == 0 else lanes - 1 - n
            at = pl.ds(pl.multiple_of(k * depth, BS), depth)
            value = values[at, :] - gain_1[at, :] * nearer - gain_2[at, :] * farther
            values[at, :] = value
            fresh.append((value, nearer))
        return tuple(fresh)

    lax.fori_loop(0, half, back, (low_next, high_next))
    for q in range(quarters):
        solved = [values[pl.ds(u * quarters + q, lanes, stride=depth), :] for u in range(variables)]
        for v in range(variables):
            total_v = right[v * variables] * solved[0]
            for u in range(1, variables):
                total_v = total_v + right[v * variables + u] * solved[u]
            turned = total_v.T
            for j in range(per_quarter):
                at = pl.ds(q * per_quarter + j, rows_i, stride=rows_j)
                piece = turned[j * rows_i : (j + 1) * rows_i]
                increment[v, at, :] = piece
                advanced[v, at, :] = filled[v, at, :] + piece


def local(
    flow_state, spectral, wave_speed, left_map, right_map,
    donor_block, receiver_block, fringe_count, fringe_weight,
):
    variables, grids, rows_i, rows_j, rows_k = flow_state.shape
    assert grids == 1 and rows_k == LANES
    total = rows_i * rows_j
    devices, capacity = donor_block.shape[1:]
    slots = devices * capacity
    flow = flow_state.reshape(variables, total, rows_k)
    rho = spectral.reshape(3, total, rows_k)
    speeds = wave_speed.reshape(-1)
    left = left_map.reshape(-1)
    right = right_map.reshape(-1)
    packed_rows = -(-variables * BS // GROUPS) * BS
    field = shape(variables, total, rows_k)
    i_plane = (variables, rows_j, rows_k)
    j_plane = (variables, rows_i, rows_k)
    axes = ("ia", "ja", "ka")

    cube_count = total // (BS * BS) * (rows_k // BS)
    depth = -(-variables * (total // LANES) // BS) * BS
    live = jnp.arange(capacity, dtype=jnp.int32)[None, :] < fringe_count[0][:, None]
    target = jnp.where(live, receiver_block[0], -1).reshape(-1)
    slot = jnp.arange(slots, dtype=jnp.int32)
    hits = target[None, :] == jnp.arange(cube_count, dtype=jnp.int32)[:, None]
    source = jnp.max(jnp.where(hits, slot[None, :], -1), axis=1)
    dma = pltpu.SemaphoreType.DMA

    def held(*dims):
        return pltpu.VMEM(dims, F32)

    whole = [held(variables, total, rows_k)]
    advanced, increment = call(
        functools.partial(step_body, axes, capacity, rows_i, rows_j),
        [field, field],
        [SMEM] * 6 + [VMEM] * 2,
        (speeds, left, right, donor_block.reshape(-1), source, fringe_weight.reshape(-1), flow, rho),
        scratch=[
            held(cube_count, packed_rows, LANES),
            held(slots, packed_rows, LANES),
            held(slots, packed_rows, LANES),
        ]
        + whole
        + whole * 4
        + [held(4, *i_plane)] * 3
        + whole * 4
        + [held(4, *j_plane)] * 3
        + [dma((devices,))] * 2
        + [dma((2, 2))] * 2
        + [
            held(variables, total + 2 * rows_j, rows_k),
            *whole * 2,
            held(2, *i_plane),
            held(2, *j_plane),
            held(2, *j_plane),
            dma((2, 4)),
        ]
        + [held(2, *i_plane)] * 5
        + [dma((3, 2))]
        + [held(2, *j_plane)] * 5
        + [dma((3, 2))]
        + whole
        + [held(rows_k * depth, LANES)] * 4,
        collective_id=0,
    )
    return advanced.reshape(flow_state.shape), increment.reshape(flow_state.shape)


def solution(mesh):
    return jax.shard_map(
        local,
        mesh=mesh,
        in_specs=(
            P(None, "ka", "ia", "ja", None),
            P(None, "ka", "ia", "ja", None),
            P(None, "ka", None),
            P("ka", None, None),
            P("ka", None, None),
            P(("ia", "ja", "ka"), None, None),
            P(("ia", "ja", "ka"), None, None),
            P(("ia", "ja", "ka"), None),
            P(None, ("ia", "ja", "ka"), None, None),
        ),
        out_specs=(P(None, "ka", "ia", "ja", None), P(None, "ka", "ia", "ja", None)),
        check_vma=False,
    )
```

profile of v0, /device:TPU:0, one launch (start us, length us, event | category | flops | bytes accessed | tf_op | source)
XLA Modules:
  0.0 73.1 jit_solution(12481189568057436637)
XLA Ops:
  0.6 0.7 fusion
  1.3 0.1 select_reduce_fusion.source
  1.4 0.7 reduce
  2.1 0.1 reshape.38.speeds
  2.2 0.7 reduce.3
  2.9 0.1 reshape.42.weights
  3.0 0.7 reduce.1
  3.7 0.1 reshape.39.left
  3.7 0.7 reduce.2
  4.4 0.1 reshape.40.right
  4.5 0.0 copy-start
  4.5 1.3 %copy-done = f32[5,1,32,16,128]{4,3,2,1,0:T(8,128)S(1)} copy-done((f32[5,1,32,16,128]{4,3,2,1,0:T(8,128)S(1)}, f32[5,1,32,16,128]{4,3,2,1,0:T(8,128)}, u32[]{:S(2)}) %copy-start) | copy-done | bytes 1310744
  5.8 0.0 copy-start.1
  5.8 1.1 %copy-done.1 = f32[3,1,32,16,128]{4,3,2,1,0:T(8,128)S(1)} copy-done((f32[3,1,32,16,128]{4,3,2,1,0:T(8,128)S(1)}, f32[3,1,32,16,128]{4,3,2,1,0:T(8,128)}, u32[]{:S(2)}) %copy-start.1) | copy-done | bytes 786456
  7.0 0.0 copy-start.2
  7.0 0.7 copy-done.2
  7.6 63.3 %shard_map.104 = (f32[5,512,128]{2,1,0:T(8,128)S(1)}, f32[5,512,128]{2,1,0:T(8,128)S(1)}) custom-call(f32[15]{0:T(128)S(1)} %reshape.38.speeds, f32[25]{0:T(128)S(1)} %reshape.39.left, f32[25]{0:T(128)S(1)} %reshape.40.right, s32[32]{0:T(128)S(1)} %bitcast.17, s32[128]{0:T(128)S(1)} %select_reduce_fusion.source, f32[96]{0:T(128)S(1)} %reshape.42.weights, ...), custom_call_target="tpu_custom_call" | custom-call | flops 4000000 | bytes 4719876 | tf_op jit(solution)/shard_map/pallas_call | solution.py:24
  71.0 1.1 %copy.17 = f32[5,1,32,16,128]{4,3,2,1,0:T(8,128)} copy(f32[5,1,32,16,128]{4,3,2,1,0:T(8,128)S(1)} %bitcast.15) | data formatting | bytes 2621440
  72.0 1.1 %copy.18 = f32[5,1,32,16,128]{4,3,2,1,0:T(8,128)} copy(f32[5,1,32,16,128]{4,3,2,1,0:T(8,128)S(1)} %bitcast.14) | data formatting | bytes 2621440
Async XLA Ops:
  4.5 1.3 %copy-start = (f32[5,1,32,16,128]{4,3,2,1,0:T(8,128)S(1)}, f32[5,1,32,16,128]{4,3,2,1,0:T(8,128)}, u32[]{:S(2)}) copy-start(f32[5,1,32,16,128]{4,3,2,1,0:T(8,128)} %param.9) | copy-start | bytes 3932164
  5.8 1.1 %copy-start.1 = (f32[3,1,32,16,128]{4,3,2,1,0:T(8,128)S(1)}, f32[3,1,32,16,128]{4,3,2,1,0:T(8,128)}, u32[]{:S(2)}) copy-start(f32[3,1,32,16,128]{4,3,2,1,0:T(8,128)} %param.10) | copy-start | bytes 2359300
  7.0 0.7 copy-start.2
where the time goes:
time: 73.4 us; the launch traced here: 73.1 us
  Pallas kernels  63.3 us (86%)
  local copies, waits for them, and re-layouts  5.54 us (8%)
  other arithmetic  3.56 us (5%)
    pallas_call x1, Pallas kernels, call(): pl.pallas_call(body, out_shape=outs, in_specs=ins, out_specs=[VMEM] * len...  63.3 us
    unnamed x8, local copies, waits for them, and re-layouts  5.22 us
    unnamed x4, other arithmetic  2.79 us

commit v1 on v0

--- a/solution.py
+++ b/solution.py
@@ -447,6 +447,8 @@
         factor_pass(direction, rows, stride, line.lower, speeds, spectral, start, gains, last)
         send_inward(line, last, start, sems.at[0], far, sems.at[1])
 
+    factor_third(rows_j, total, speeds, spectral, *thirds[:6])
+
     def end(step, carry):
         cubes(step, (me + step) % devices, (me + devices - step) % devices).wait_recv()
         return carry
@@ -564,19 +566,24 @@
             def _():
                 line.send(solved, nexts, sems.at[2], line.outer).wait_send()
 
-    finish(rows_j, speeds, right, lines, spectral, filled, advanced, increment, *thirds)
-
-
-def finish(
-    rows_j, speeds, right, lines, spectral, filled,
-    advanced, increment, values, coupling, gain_1, gain_2,
-):
-    variables, total, lanes = lines.shape
+    finish(rows_j, right, lines, filled, advanced, increment, *thirds)
+
+
+def turned_rows(quarter, quarters, v, lanes, depth):
+    return pl.ds(v * quarters + quarter, lanes, stride=depth)
+
+
+def both_ends(n, lanes, depth):
+    return [pl.ds(pl.multiple_of(k * depth, BS), depth) for k in (n, lanes - 1 - n)]
+
+
+def factor_third(rows_j, total, speeds, spectral, values, inverse, coupled, gain_1, gain_2, last):
+    lanes = spectral.shape[2]
     rows_i = total // rows_j
     quarters = total // LANES
     per_quarter = LANES // rows_i
     depth = values.shape[0] // lanes
-
+    count = speeds.shape[0] // 3
     for q in range(quarters):
         rho = jnp.concatenate(
             [
@@ -585,58 +592,77 @@
             ],
             axis=0,
         ).T
+        for v in range(count):
+            inverse[turned_rows(q, quarters, v, lanes, depth), :] = speeds[2 * count + v] * rho
+    for spare in range(count * quarters, depth):
+        at = pl.ds(spare, lanes, stride=depth)
+        inverse[at, :] = jnp.zeros((lanes, lanes), F32)
+        values[at, :] = jnp.zeros((lanes, lanes), F32)
+
+    last[...] = jnp.zeros(last.shape, F32)
+    begin = tuple(tuple(last[side, m] for m in range(4)) for side in range(2))
+
+    def one(n, carry):
+        fresh = []
+        for side, at in enumerate(both_ends(n, lanes, depth)):
+            older_first, older_second, last_first, last_second = carry[side]
+            a, b, c, d = eliminate(inverse[at, :], older_first, older_second, last_first, last_second)
+            inverse[at, :] = a
+            coupled[at, :] = b
+            gain_1[at, :] = c
+            gain_2[at, :] = d
+            fresh.append((last_first, last_second, c, d))
+        return tuple(fresh)
+
+    ends = lax.fori_loop(0, lanes // 2, one, begin)
+    for side in range(2):
+        for m in range(4):
+            last[side, m] = ends[side][m]
+
+
+def finish(
+    rows_j, right, lines, filled, advanced, increment, values, inverse, coupled, gain_1, gain_2, last, carry
+):
+    variables, total, lanes = lines.shape
+    rows_i = total // rows_j
+    quarters = total // LANES
+    per_quarter = LANES // rows_i
+    depth = values.shape[0] // lanes
+    for q in range(quarters):
         for v in range(variables):
-            at = pl.ds(v * quarters + q, lanes, stride=depth)
-            coupling[at, :] = speeds[2 * variables + v] * rho
+            at = turned_rows(q, quarters, v, lanes, depth)
             values[at, :] = lines[v, q * LANES : (q + 1) * LANES, :].T
-    for spare in range(variables * quarters, depth):
-        at = pl.ds(spare, lanes, stride=depth)
-        coupling[at, :] = jnp.zeros((lanes, lanes), F32)
-        values[at, :] = jnp.zeros((lanes, lanes), F32)
 
     half = lanes // 2
-    gain_1[:depth, :] = jnp.zeros((depth, lanes), F32)
-    zero = gain_1[:depth, :]
-
-    def ahead(n, carry):
+    carry[...] = jnp.zeros(carry.shape, F32)
+
+    def ahead(n, state):
         fresh = []
-        for side in range(2):
-            older_first, older_second, older, last_first, last_second, newer = carry[side]
-            k = n if side == 0 else lanes - 1 - n
-            at = pl.ds(pl.multiple_of(k * depth, BS), depth)
-            inverse, coupled, one, two = eliminate(
-                coupling[at, :], older_first, older_second, last_first, last_second
-            )
-            value = values[at, :] * inverse - two * older - coupled * newer
-            gain_1[at, :] = one
-            gain_2[at, :] = two
+        for side, at in enumerate(both_ends(n, lanes, depth)):
+            older, newer = state[side]
+            value = values[at, :] * inverse[at, :] - gain_2[at, :] * older - coupled[at, :] * newer
             values[at, :] = value
-            fresh.append((last_first, last_second, newer, one, two, value))
+            fresh.append((newer, value))
         return tuple(fresh)
 
-    low, high = lax.fori_loop(0, half, ahead, ((zero,) * 6,) * 2)
-
-    def ends(side):
-        return [side[0], side[1], side[3], side[4]], [side[2], side[5]]
-
-    low_next = meet(*ends(low), *ends(high))
-    high_next = meet(*ends(high), *ends(low))
-
-    def back(step, carry):
+    begin = tuple((carry[side, 0], carry[side, 1]) for side in range(2))
+    low, high = lax.fori_loop(0, half, ahead, begin, unroll=2)
+    gains = [[last[side, m] for m in range(4)] for side in range(2)]
+    low_next = meet(gains[0], low, gains[1], high)
+    high_next = meet(gains[1], high, gains[0], low)
+
+    def back(step, state):
         fresh = []
-        for side in range(2):
-            nearer, farther = carry[side]
-            n = half - 1 - step
-            k = n if side == 0 else lanes - 1 - n
-            at = pl.ds(pl.multiple_of(k * depth, BS), depth)
+        for side, at in enumerate(both_ends(half - 1 - step, lanes, depth)):
+            nearer, farther = state[side]
             value = values[at, :] - gain_1[at, :] * nearer - gain_2[at, :] * farther
             values[at, :] = value
             fresh.append((value, nearer))
         return tuple(fresh)
 
-    lax.fori_loop(0, half, back, (low_next, high_next))
+    lax.fori_loop(0, half, back, (low_next, high_next), unroll=2)
     for q in range(quarters):
-        solved = [values[pl.ds(u * quarters + q, lanes, stride=depth), :] for u in range(variables)]
+        solved = [values[turned_rows(q, quarters, u, lanes, depth), :] for u in range(variables)]
         for v in range(variables):
             total_v = right[v * variables] * solved[0]
             for u in range(1, variables):
@@ -712,7 +738,8 @@
         + [held(2, *j_plane)] * 5
         + [dma((3, 2))]
         + whole
-        + [held(rows_k * depth, LANES)] * 4,
+        + [held(rows_k * depth, LANES)] * 5
+        + [held(2, 4, depth, LANES), held(2, 2, depth, LANES)],
         collective_id=0,
     )
     return advanced.reshape(flow_state.shape), increment.reshape(flow_state.shape)

time: 73.4 us -> 74.1 us (level)
  no operation moved by 1% of the time
where the time goes in v1:
time: 74.1 us; the launch traced here: 73.8 us
  Pallas kernels  64 us (86%)
  local copies, waits for them, and re-layouts  5.54 us (7%)
  other arithmetic  3.56 us (5%)
    pallas_call x1, Pallas kernels, call(): pl.pallas_call(body, out_shape=outs, in_specs=ins, out_specs=[VMEM] * len...  64 us
    unnamed x8, local copies, waits for them, and re-layouts  5.22 us
    unnamed x4, other arithmetic  2.79 us

profile of v1, /device:TPU:0, one launch (start us, length us, event | category | flops | bytes accessed | tf_op | source)
XLA Modules:
  0.0 73.8 jit_solution(7039176830676809370)
XLA Ops:
  0.6 0.7 fusion
  1.3 0.1 select_reduce_fusion.source
  1.4 0.7 reduce
  2.1 0.1 reshape.38.speeds
  2.2 0.7 reduce.3
  2.9 0.1 reshape.42.weights
  3.0 0.7 reduce.1
  3.7 0.1 reshape.39.left
  3.7 0.7 reduce.2
  4.4 0.1 reshape.40.right
  4.5 0.0 copy-start
  4.5 1.3 %copy-done = f32[5,1,32,16,128]{4,3,2,1,0:T(8,128)S(1)} copy-done((f32[5,1,32,16,128]{4,3,2,1,0:T(8,128)S(1)}, f32[5,1,32,16,128]{4,3,2,1,0:T(8,128)}, u32[]{:S(2)}) %copy-start) | copy-done | bytes 1310744
  5.8 0.0 copy-start.1
  5.8 1.1 %copy-done.1 = f32[3,1,32,16,128]{4,3,2,1,0:T(8,128)S(1)} copy-done((f32[3,1,32,16,128]{4,3,2,1,0:T(8,128)S(1)}, f32[3,1,32,16,128]{4,3,2,1,0:T(8,128)}, u32[]{:S(2)}) %copy-start.1) | copy-done | bytes 786456
  7.0 0.0 copy-start.2
  7.0 0.7 copy-done.2
  7.6 64.0 %shard_map.104 = (f32[5,512,128]{2,1,0:T(8,128)S(1)}, f32[5,512,128]{2,1,0:T(8,128)S(1)}) custom-call(f32[15]{0:T(128)S(1)} %reshape.38.speeds, f32[25]{0:T(128)S(1)} %reshape.39.left, f32[25]{0:T(128)S(1)} %reshape.40.right, s32[32]{0:T(128)S(1)} %bitcast.17, s32[128]{0:T(128)S(1)} %select_reduce_fusion.source, f32[96]{0:T(128)S(1)} %reshape.42.weights, ...), custom_call_target="tpu_custom_call" | custom-call | flops 4000000 | bytes 4719876 | tf_op jit(solution)/shard_map/pallas_call | solution.py:24
  71.7 1.1 %copy.17 = f32[5,1,32,16,128]{4,3,2,1,0:T(8,128)} copy(f32[5,1,32,16,128]{4,3,2,1,0:T(8,128)S(1)} %bitcast.15) | data formatting | bytes 2621440
  72.7 1.1 %copy.18 = f32[5,1,32,16,128]{4,3,2,1,0:T(8,128)} copy(f32[5,1,32,16,128]{4,3,2,1,0:T(8,128)S(1)} %bitcast.14) | data formatting | bytes 2621440
Async XLA Ops:
  4.5 1.3 %copy-start = (f32[5,1,32,16,128]{4,3,2,1,0:T(8,128)S(1)}, f32[5,1,32,16,128]{4,3,2,1,0:T(8,128)}, u32[]{:S(2)}) copy-start(f32[5,1,32,16,128]{4,3,2,1,0:T(8,128)} %param.9) | copy-start | bytes 3932164
  5.8 1.1 %copy-start.1 = (f32[3,1,32,16,128]{4,3,2,1,0:T(8,128)S(1)}, f32[3,1,32,16,128]{4,3,2,1,0:T(8,128)}, u32[]{:S(2)}) copy-start(f32[3,1,32,16,128]{4,3,2,1,0:T(8,128)} %param.10) | copy-start | bytes 2359300
  7.0 0.7 copy-start.2
